TPU v7x, 512 devices: a whole 4x4x16 slice. The times are simulated.
512 devices in a mesh: expert: 32 (over z, core), tensor: 16 (over y, x).
Axes of the slice: x: 4, y: 4, z: 16, core: 2. Of those that a mesh axis runs over, the one named last changes fastest.
Arguments:
- hidden_in: bfloat16 [4096, 4096], P('expert', 'tensor'), may hold values from -92 to 92
- norm_gain: float32 [4096], P('tensor'), may hold values from 0.5 to 1.5
- expert_ids: int32 [4096, 8], P('expert'), may hold values from 0 to 63, all different within a row; in each aligned block of 128 rows (0 to 127, 128 to 255, ...) at most 24 rows name the same one
- route_weights: float32 [4096, 8], P('expert'), may hold values from 0.05 to 0.5
- w_gate: bfloat16 [64, 1536, 4096], P('expert', 'tensor'), may hold values from -0.09375 to 0.09375
- w_up: bfloat16 [64, 1536, 4096], P('expert', 'tensor'), may hold values from -0.09375 to 0.09375
- w_down: bfloat16 [64, 1536, 4096], P('expert', 'tensor'), may hold values from -0.15625 to 0.15625
Outputs:
- moe_out: bfloat16 [4096, 4096], P('expert', 'tensor')
Inputs may be any that keep to these rules, and one draw needn't show every extreme that they name: `expert_ids`: in each aligned block of 128 rows (the rows of one index of the expert axis) no expert is named by more than 24 rows, a bound that some block reaches.
All inputs are finite; a program needn't handle non-finite values.
Results may differ from a plain program's by a relative error of at most 0.019.
Values may be sent and summed in bfloat16 or wider, within the bound.
A program may use at most 128 MiB of HBM per device.

v0:
```python
import jax
import jax.numpy as jnp
from jax import lax
from jax.sharding import PartitionSpec as P

D = 4096
epsilon = 1e-06


def body(hidden_in, norm_gain, expert_ids, route_weights, w_gate, w_up, w_down):
    tokens_here = hidden_in.shape[0]
    choices_count = expert_ids.shape[1]
    exp_local = w_gate.shape[0]
    groups = lax.axis_size("expert")
    experts_all = exp_local * groups
    capacity = min(tokens_here, 3 * tokens_here * choices_count // (2 * experts_all))
    widened = hidden_in.astype(jnp.float32)
    squares = lax.psum(jnp.sum(widened * widened, axis=1), "tensor")
    normed = (widened * lax.rsqrt(squares / D + epsilon)[:, None] * norm_gain[None, :]).astype(
        jnp.bfloat16
    )
    routing = jnp.concatenate([expert_ids.astype(jnp.float32), route_weights], axis=1)
    routing = lax.all_gather(routing.T, "expert", axis=0, tiled=False)
    tokens_all = lax.all_gather(normed, "expert", axis=0, tiled=False)
    first = (lax.axis_index("expert") * exp_local).astype(jnp.float32)
    named = (
        routing[:, None, :choices_count, :]
        == first + jnp.arange(exp_local, dtype=jnp.float32)[None, :, None, None]
    )
    chosen = jnp.any(named, axis=2)
    scale = jnp.sum(jnp.where(named, routing[:, None, choices_count:, :], 0.0), axis=2)
    step = jnp.arange(tokens_here, dtype=jnp.int32)
    earlier = (step[:, None] < step[None, :]).astype(jnp.bfloat16)
    position = jnp.einsum(
        "bjs,st->bjt", chosen.astype(jnp.bfloat16), earlier, preferred_element_type=jnp.float32
    )
    slot = jnp.arange(capacity, dtype=jnp.float32)
    select = (
        (position[:, :, None, :] == slot[None, None, :, None]) & chosen[:, :, None, :]
    ).astype(jnp.bfloat16)
    rows = jnp.einsum(
        "bjst,btd->bjsd", select, tokens_all, preferred_element_type=jnp.float32
    ).astype(jnp.bfloat16)
    rows = rows.transpose(1, 0, 2, 3).reshape(exp_local, groups * capacity, -1)
    piece = lax.all_gather(rows, "tensor", axis=2, tiled=True)
    gate_add = jnp.einsum("erd,efd->erf", piece, w_gate, preferred_element_type=jnp.float32)
    up_add = jnp.einsum("erd,efd->erf", piece, w_up, preferred_element_type=jnp.float32)
    inner = (jax.nn.silu(gate_add) * up_add).astype(jnp.bfloat16)
    partials = jnp.einsum("erf,efd->erd", inner, w_down, preferred_element_type=jnp.float32).astype(
        jnp.bfloat16
    )
    summed = lax.psum_scatter(partials, "tensor", scatter_dimension=2, tiled=True)
    summed = summed.reshape(exp_local, groups, capacity, -1)
    back = jnp.einsum("bjst,jbsd->bjtd", select, summed, preferred_element_type=jnp.float32)
    weighted = jnp.sum(back * scale[:, :, :, None], axis=1).astype(jnp.bfloat16)
    return lax.psum_scatter(weighted, "expert", scatter_dimension=0, tiled=False)


def solution(mesh):
    placed = (
        P("expert", "tensor"),
        P("tensor"),
        P("expert", None),
        P("expert", None),
        P("expert", "tensor", None),
        P("expert", "tensor", None),
        P("expert", "tensor", None),
    )
    return jax.shard_map(
        body, mesh=mesh, in_specs=placed, out_specs=P("expert", "tensor"), check_vma=False
    )
```

profile of v0, /device:TPU:18, one launch (start us, length us, event | category | flops | bytes accessed | tf_op | source)
XLA Modules:
  0.0 491.3 jit_solution(8719006843433217021)
XLA Ops:
  6.5 0.0 copy-start
  6.5 0.0 all-gather.7.cloned.1.call-start
  6.5 1.1 fusion.17
  7.6 31.1 %psum.7 = f32[128]{0:T(128)S(1)} all-reduce(f32[128]{0:T(128)S(1)} %fusion.17), channel_id=1, replica_groups=mesh['expert'=32,'tensor'=16] {'tensor'}, use_global_device_ids=true, to_apply=%region_2.0 | all-reduce | flops 128 | bytes 1024 | tf_op jit(solution)/shard_map/psum | solution.py:18
  38.8 1.6 fusion.19
  40.3 0.0 all-gather.7.cloned.1.call-update
  40.3 0.0 all-gather.5.cloned.1.call-start
  40.4 0.7 convert_element_type.31
  41.1 0.7 maximum_bitcast_fusion
  41.8 37.0 %all-gather = f32[512,128]{1,0:T(8,128)S(1)} all-gather(f32[16,128]{1,0:T(8,128)S(1)} %maximum_bitcast_fusion), channel_id=2, replica_groups=mesh['expert'=32,'tensor'=16] {'expert'}, dimensions={0}, use_global_device_ids=true | all-gather | bytes 270336 | tf_op jit(solution)/shard_map/all_gather | solution.py:23
  78.8 0.2 compare_reduce_fusion
  79.0 0.1 fusion.21
  79.2 41.8 %all-gather.7.cloned.1.call-done = bf16[4096,256]{1,0:T(8,128)(2,1)} async-done(((bf16[128,256]{1,0:T(8,128)(2,1)}), bf16[4096,256]{1,0:T(8,128)(2,1)}) %all-gather.7.cloned.1.call-update) | async-done | bytes 2097168 | tf_op jit(solution)/shard_map/all_gather | solution.py:24
  121.0 2.0 fusion
  123.0 1.0 copy.17
  124.0 0.0 all-gather.5.cloned.1.call-update
  124.0 0.0 reduce-scatter.3.cloned.1.call-start
  124.1 110.4 %all-gather.5.cloned.1.call-done = bf16[2,768,4096]{2,1,0:T(8,128)(2,1)} async-done(((bf16[2,768,256]{2,1,0:T(8,128)(2,1)}), bf16[2,768,4096]{2,1,0:T(8,128)(2,1)}) %all-gather.5.cloned.1.call-update) | async-done | bytes 12582928 | tf_op jit(solution)/shard_map/all_gather | solution.py:45
  234.4 9.0 %fusion.26 = f32[2,768,96]{1,2,0:T(8,128)S(1)} fusion(bf16[2,768,4096]{2,1,0:T(8,128)(2,1)} %all-gather.5.cloned.1.call-done, bf16[2,96,4096]{2,1,0:T(8,128)(2,1)} %param.11), kind=kOutput, calls=%fused_computation.36 | convolution fusion | flops 1207959552 | bytes 14745600 | tf_op jit(solution)/shard_map/erd,efd->erf/dot_general | solution.py:46
  243.4 0.0 copy-done
  243.4 15.3 %convolution_convert_fusion = bf16[2,768,4096]{2,1,0:T(8,128)(2,1)} fusion(bf16[2,96,4096]{2,1,0:T(8,128)(2,1)S(1)} %copy-done, bf16[2,768,4096]{2,1,0:T(8,128)(2,1)} %all-gather.5.cloned.1.call-done, bf16[2,96,4096]{2,1,0:T(8,128)(2,1)} %param.12, f32[2,768,96]{1,2,0:T(8,128)S(1)} %fusion.26), kind=kOutput, calls=%fused_computation | convolution fusion | flops 2423095296 | bytes 28901376 | tf_op jit(solution)/shard_map/erf,efd->erd/dot_general | solution.py:49
  258.7 0.0 reduce-scatter.3.cloned.1.call-update
  258.8 0.0 reduce-scatter.5.cloned.1.call-start
  258.8 0.2 fusion.16
  259.0 109.0 %reduce-scatter.3.cloned.1.call-done = bf16[2,768,256]{2,1,0:T(8,128)(2,1)} async-done(((bf16[2,768,4096]{2,1,0:T(8,128)(2,1)}), bf16[2,768,256]{2,1,0:T(8,128)(2,1)}) %reduce-scatter.3.cloned.1.call-update) | async-done | bytes 786448 | tf_op jit(solution)/shard_map/reduce_scatter | solution.py:52
  368.0 5.3 %multiply_reduce_fusion = bf16[32,128,256]{2,1,0:T(8,128)(2,1)} fusion(f32[32,2,128]{2,1,0:T(2,128)S(1)} %fusion.16, bf16[2,32,24,256]{3,2,1,0:T(8,128)(2,1)} %bitcast.25, f32[32,2,128]{2,1,0:T(2,128)S(1)} %copy.16, pred[32,2,128]{2,1,0:T(4,128)(4,1)S(1)} %compare_reduce_fusion), kind=kOutput, calls=%fused_computation.1 | convolution fusion | flops 104202240 | bytes 2957312 | tf_op jit(solution)/shard_map/bjst,jbsd->bjtd/dot_general | solution.py:54
  373.3 0.0 reduce-scatter.5.cloned.1.call-update
  373.3 111.5 %reduce-scatter.5.cloned.1.call-done = bf16[1,128,256]{2,1,0:T(8,128)(2,1)} async-done(((bf16[32,128,256]{2,1,0:T(8,128)(2,1)}), bf16[1,128,256]{2,1,0:T(8,128)(2,1)}) %reduce-scatter.5.cloned.1.call-update) | async-done | bytes 65552 | tf_op jit(solution)/shard_map/reduce_scatter | solution.py:56
  (4 shorter events, 0.1 us)
Async XLA Ops:
  6.5 236.9 %copy-start = (bf16[2,96,4096]{2,1,0:T(8,128)(2,1)S(1)}, bf16[2,96,4096]{2,1,0:T(8,128)(2,1)}, u32[]{:S(2)}) copy-start(bf16[2,96,4096]{2,1,0:T(8,128)(2,1)} %param.13) | copy-start | bytes 4718596
  6.5 114.5 %all-gather.7.cloned.1.call-start = ((), (), s32[]{:S(2)}) async-start(), calls=%async_computation.5 | async-start | bytes 2162688 | tf_op jit(solution)/shard_map/all_gather | solution.py:24
  40.3 194.1 %all-gather.5.cloned.1.call-start = ((), (), s32[]{:S(2)}) async-start(), calls=%async_computation.2 | async-start | bytes 13369344 | tf_op jit(solution)/shard_map/all_gather | solution.py:45
  124.0 243.9 %reduce-scatter.3.cloned.1.call-start = ((), (), s32[]{:S(2)}) async-start(), calls=%async_computation.3 | async-start | bytes 13369344 | tf_op jit(solution)/shard_map/reduce_scatter | solution.py:52
  258.8 226.0 %reduce-scatter.5.cloned.1.call-start = ((), (), s32[]{:S(2)}) async-start(), calls=%async_computation.4 | async-start | bytes 2162688 | tf_op jit(solution)/shard_map/reduce_scatter | solution.py:56
Sparse Core Ops, SparseCore 0:
  40.5 80.4 all-gather.6
  124.1 110.2 all-gather.4
  258.9 109.0 reduce-scatter.2
  373.4 111.3 reduce-scatter.4
where the time goes:
time: 492 us; the launch traced here: 491 us
  waiting for transfers between devices  373 us (76%)
  blocking collectives  68.2 us (14%)
  matrix products  31.7 us (6%)
  between operations  13.2 us (3%)
    reduce_scatter x1, waiting for transfers between devices, body(): lax.psum_scatter(weighted, 'expert', scatter_dimension=0, tiled=False)  111 us
    all_gather x1, waiting for transfers between devices, body(): piece = lax.all_gather(rows, 'tensor', axis=2, tiled=True)  110 us
    reduce_scatter x1, waiting for transfers between devices, body(): lax.psum_scatter(partials, 'tensor', scatter_dimension=2, tiled=True)  109 us
    all_gather x1, waiting for transfers between devices, body(): tokens_all = lax.all_gather(normed, 'expert', axis=0, tiled=False)  41.8 us
    all_gather x1, blocking collectives, body(): routing = lax.all_gather(routing.T, 'expert', axis=0, tiled=False)  37 us
    psum x1, blocking collectives, body(): squares = lax.psum(jnp.sum(widened * widened, axis=1), 'tensor')  31.1 us
    dot_general x1, matrix products, body(): jnp.einsum('erf,efd->erd', inner, w_down, preferred_element_type=jnp.floa...  15.3 us
  transfers between devices with their start and end apart: 4, of which 4 were waited for; matrix products, arithmetic and copies ran while one was open for 0% of the time, Pallas kernels for 0%

commit v1 on v0

--- a/solution.py
+++ b/solution.py
@@ -8,6 +8,14 @@
 
 
 def body(hidden_in, norm_gain, expert_ids, route_weights, w_gate, w_up, w_down):
+
+    def pass_the_signs(view):
+        a_name = "tensor"
+        p_count = jax.lax.axis_size(a_name)
+        pile = [p_count if k0 == 2 else 1 for k0 in range(view.ndim)]
+        res = jnp.tile(view, pile)
+        return jax.lax.all_to_all(res, a_name, split_axis=2, concat_axis=2, tiled=True)
+
     tokens_here = hidden_in.shape[0]
     choices_count = expert_ids.shape[1]
     exp_local = w_gate.shape[0]
@@ -42,7 +50,7 @@
         "bjst,btd->bjsd", select, tokens_all, preferred_element_type=jnp.float32
     ).astype(jnp.bfloat16)
     rows = rows.transpose(1, 0, 2, 3).reshape(exp_local, groups * capacity, -1)
-    piece = lax.all_gather(rows, "tensor", axis=2, tiled=True)
+    piece = pass_the_signs(rows)
     gate_add = jnp.einsum("erd,efd->erf", piece, w_gate, preferred_element_type=jnp.float32)
     up_add = jnp.einsum("erd,efd->erf", piece, w_up, preferred_element_type=jnp.float32)
     inner = (jax.nn.silu(gate_add) * up_add).astype(jnp.bfloat16)

time: 492 us -> 564 us (1.15)
  the two profiles are of different devices: /device:TPU:18 before, /device:TPU:2 now
where the time goes in v1:
time: 564 us; the launch traced here: 563 us
  waiting for transfers between devices  250 us (44%)
  blocking collectives  221 us (39%)
  local copies, waits for them, and re-layouts  42.9 us (8%)
  matrix products  31.7 us (6%)
  between operations  13.2 us (2%)
    all_to_all x1, blocking collectives, pass_the_signs(): jax.lax.all_to_all(res, a_name, split_axis=2, concat_axis=2, tiled=True)  147 us
    reduce_scatter x1, waiting for transfers between devices, body(): lax.psum_scatter(weighted, 'expert', scatter_dimension=0, tiled=False)  110 us
    reduce_scatter x1, waiting for transfers between devices, body(): lax.psum_scatter(partials, 'tensor', scatter_dimension=2, tiled=True)  103 us
    psum x1, blocking collectives, body(): squares = lax.psum(jnp.sum(widened * widened, axis=1), 'tensor')  41.4 us
    all_gather x1, waiting for transfers between devices, body(): tokens_all = lax.all_gather(normed, 'expert', axis=0, tiled=False)  36.6 us
    all_gather x1, blocking collectives, body(): routing = lax.all_gather(routing.T, 'expert', axis=0, tiled=False)  32.2 us
    all_to_all x1, local copies, waits for them, and re-layouts, pass_the_signs(): jax.lax.all_to_all(res, a_name, split_axis=2, concat_axis=2, tiled=True)  31.1 us
    dot_general x1, matrix products, body(): jnp.einsum('erf,efd->erd', inner, w_down, preferred_element_type=jnp.floa...  15.3 us
  transfers between devices with their start and end apart: 3, of which 3 were waited for; matrix products, arithmetic and copies ran while one was open for 0% of the time, Pallas kernels for 0%

profile of v1, /device:TPU:2, one launch (start us, length us, event | category | flops | bytes accessed | tf_op | source)
XLA Modules:
  0.0 562.8 jit_solution(14428305000905469262)
XLA Ops:
  6.5 0.0 copy-start
  6.5 0.0 all-gather.4.cloned.1.call-start
  6.5 1.1 fusion.17
  7.6 41.4 %psum.7 = f32[128]{0:T(128)S(1)} all-reduce(f32[128]{0:T(128)S(1)} %fusion.17), channel_id=1, replica_groups=mesh['expert'=32,'tensor'=16] {'tensor'}, use_global_device_ids=true, to_apply=%region_2.0 | all-reduce | flops 128 | bytes 1024 | tf_op jit(solution)/shard_map/psum | solution.py:26
  49.0 1.6 fusion.19
  50.5 0.0 all-gather.4.cloned.1.call-update
  50.6 0.0 reduce-scatter.3.cloned.1.call-start
  50.6 0.7 convert_element_type.31
  51.3 0.7 maximum_bitcast_fusion
  52.0 32.2 %all-gather = f32[512,128]{1,0:T(8,128)S(1)} all-gather(f32[16,128]{1,0:T(8,128)S(1)} %maximum_bitcast_fusion), channel_id=2, replica_groups=mesh['expert'=32,'tensor'=16] {'expert'}, dimensions={0}, use_global_device_ids=true | all-gather | bytes 270336 | tf_op jit(solution)/shard_map/all_gather | solution.py:31
  84.3 0.2 compare_reduce_fusion
  84.4 0.1 fusion.21
  84.6 36.6 %all-gather.4.cloned.1.call-done = bf16[4096,256]{1,0:T(8,128)(2,1)} async-done(((bf16[128,256]{1,0:T(8,128)(2,1)}), bf16[4096,256]{1,0:T(8,128)(2,1)}) %all-gather.4.cloned.1.call-update) | async-done | bytes 2097168 | tf_op jit(solution)/shard_map/all_gather | solution.py:32
  121.2 2.0 fusion
  123.2 0.1 copy.24
  123.3 0.8 copy.25
  124.1 10.9 %tile.11 = bf16[2,768,16,256]{1,0,3,2:T(2,128)(2,1)S(1)} broadcast(bf16[2,768,256]{1,0,2:T(2,128)(2,1)S(1)} %copy.25), dimensions={0,1,3} | broadcast | bytes 13369344 | tf_op jit(solution)/shard_map/tile | solution.py:16
  135.0 146.9 %all_to_all.5 = bf16[2,768,4096]{1,0,2:T(2,128)(2,1)} all-to-all(bf16[2,768,4096]{1,0,2:T(2,128)(2,1)S(1)} %bitcast.23), channel_id=1, replica_groups=mesh['expert'=32,'tensor'=16] {'tensor'}, dimensions={2} | all-to-all | bytes 25165824 | tf_op jit(solution)/shard_map/all_to_all | solution.py:17
  281.9 31.1 %copy.26 = bf16[2,768,4096]{2,1,0:T(8,128)(2,1)} copy(bf16[2,768,4096]{1,0,2:T(2,128)(2,1)} %all_to_all.5) | data formatting | bytes 25165824 | tf_op jit(solution)/shard_map/all_to_all | solution.py:17
  313.0 9.0 %fusion.26 = f32[2,768,96]{1,2,0:T(8,128)S(1)} fusion(bf16[2,768,4096]{2,1,0:T(8,128)(2,1)} %copy.26, bf16[2,96,4096]{2,1,0:T(8,128)(2,1)} %param.11), kind=kOutput, calls=%fused_computation.36 | convolution fusion | flops 1207959552 | bytes 14745600 | tf_op jit(solution)/shard_map/erd,efd->erf/dot_general | solution.py:54
  322.0 0.0 copy-done
  322.0 15.3 %convolution_convert_fusion = bf16[2,768,4096]{2,1,0:T(8,128)(2,1)} fusion(bf16[2,96,4096]{2,1,0:T(8,128)(2,1)S(1)} %copy-done, bf16[2,768,4096]{2,1,0:T(8,128)(2,1)} %copy.26, bf16[2,96,4096]{2,1,0:T(8,128)(2,1)} %param.12, f32[2,768,96]{1,2,0:T(8,128)S(1)} %fusion.26), kind=kOutput, calls=%fused_computation | convolution fusion | flops 2423095296 | bytes 28901376 | tf_op jit(solution)/shard_map/erf,efd->erd/dot_general | solution.py:57
  337.3 0.0 reduce-scatter.3.cloned.1.call-update
  337.3 0.0 reduce-scatter.5.cloned.1.call-start
  337.4 0.2 fusion.16
  337.6 103.4 %reduce-scatter.3.cloned.1.call-done = bf16[2,768,256]{2,1,0:T(8,128)(2,1)} async-done(((bf16[2,768,4096]{2,1,0:T(8,128)(2,1)}), bf16[2,768,256]{2,1,0:T(8,128)(2,1)}) %reduce-scatter.3.cloned.1.call-update) | async-done | bytes 786448 | tf_op jit(solution)/shard_map/reduce_scatter | solution.py:60
  440.9 5.3 multiply_reduce_fusion
  446.2 0.0 reduce-scatter.5.cloned.1.call-update
  446.3 110.0 %reduce-scatter.5.cloned.1.call-done = bf16[1,128,256]{2,1,0:T(8,128)(2,1)} async-done(((bf16[32,128,256]{2,1,0:T(8,128)(2,1)}), bf16[1,128,256]{2,1,0:T(8,128)(2,1)}) %reduce-scatter.5.cloned.1.call-update) | async-done | bytes 65552 | tf_op jit(solution)/shard_map/reduce_scatter | solution.py:64
  (4 shorter events, 0.1 us)
Async XLA Ops:
  6.5 315.4 %copy-start = (bf16[2,96,4096]{2,1,0:T(8,128)(2,1)S(1)}, bf16[2,96,4096]{2,1,0:T(8,128)(2,1)}, u32[]{:S(2)}) copy-start(bf16[2,96,4096]{2,1,0:T(8,128)(2,1)} %param.13) | copy-start | bytes 4718596
  6.5 114.7 %all-gather.4.cloned.1.call-start = ((), (), s32[]{:S(2)}) async-start(), calls=%async_computation.5 | async-start | bytes 2162688 | tf_op jit(solution)/shard_map/all_gather | solution.py:32
  50.6 390.4 %reduce-scatter.3.cloned.1.call-start = ((), (), s32[]{:S(2)}) async-start(), calls=%async_computation.3 | async-start | bytes 13369344 | tf_op jit(solution)/shard_map/reduce_scatter | solution.py:60
  337.3 218.9 %reduce-scatter.5.cloned.1.call-start = ((), (), s32[]{:S(2)}) async-start(), calls=%async_computation.4 | async-start | bytes 2162688 | tf_op jit(solution)/shard_map/reduce_scatter | solution.py:64
Sparse Core Ops, SparseCore 0:
  50.7 70.4 all-gather.3
  337.5 103.4 reduce-scatter.2
  446.4 109.8 reduce-scatter.4

commit v2 on v0

--- a/solution.py
+++ b/solution.py
@@ -15,7 +15,8 @@
     experts_all = exp_local * groups
     capacity = min(tokens_here, 3 * tokens_here * choices_count // (2 * experts_all))
     widened = hidden_in.astype(jnp.float32)
-    squares = lax.psum(jnp.sum(widened * widened, axis=1), "tensor")
+    time_digits = lambda z, shard_axis: lax.all_gather(z, shard_axis).sum(axis=0)
+    squares = time_digits(jnp.sum(widened * widened, axis=1), "tensor")
     normed = (widened * lax.rsqrt(squares / D + epsilon)[:, None] * norm_gain[None, :]).astype(
         jnp.bfloat16
     )

time: 492 us -> 475 us (0.965)
  the two profiles are of different devices: /device:TPU:18 before, /device:TPU:14 now
where the time goes in v2:
time: 475 us
  waiting for transfers between devices  368 us (77%)
  blocking collectives  56.3 us (12%)
  matrix products  31.7 us (7%)
  between operations  13.2 us (3%)
    reduce_scatter x1, waiting for transfers between devices, body(): lax.psum_scatter(weighted, 'expert', scatter_dimension=0, tiled=False)  111 us
    all_gather x1, waiting for transfers between devices, body(): piece = lax.all_gather(rows, 'tensor', axis=2, tiled=True)  110 us
    reduce_scatter x1, waiting for transfers between devices, body(): lax.psum_scatter(partials, 'tensor', scatter_dimension=2, tiled=True)  109 us
    all_gather x1, waiting for transfers between devices, body(): tokens_all = lax.all_gather(normed, 'expert', axis=0, tiled=False)  37.3 us
    all_gather x1, blocking collectives, body(): routing = lax.all_gather(routing.T, 'expert', axis=0, tiled=False)  36.2 us
    all_gather x1, blocking collectives, body(): lax.all_gather(z, shard_axis).sum(axis=0)  20.1 us
    dot_general x1, matrix products, body(): jnp.einsum('erf,efd->erd', inner, w_down, preferred_element_type=jnp.floa...  15.3 us
  transfers between devices with their start and end apart: 4, of which 4 were waited for; matrix products, arithmetic and copies ran while one was open for 0% of the time, Pallas kernels for 0%

profile of v2, /device:TPU:14, one launch (start us, length us, event | category | flops | bytes accessed | tf_op | source)
XLA Modules:
  0.0 474.6 jit_solution(1816265366170456552)
XLA Ops:
  6.5 0.0 copy-start
  6.5 0.0 all-gather.9.cloned.1.call-start
  6.5 1.1 fusion.17
  7.6 20.1 %all-gather.3 = f32[16,1,128]{2,1,0:T(1,128)S(1)} all-gather(f32[1,1,128]{2,1,0:T(1,128)S(1)} %bitcast.26), channel_id=3, replica_groups=mesh['expert'=32,'tensor'=16] {'tensor'}, dimensions={0}, use_global_device_ids=true | all-gather | bytes 8704 | tf_op jit(solution)/shard_map/all_gather | solution.py:18
  27.8 1.6 fusion.19
  29.3 0.0 all-gather.9.cloned.1.call-update
  29.3 0.0 all-gather.7.cloned.1.call-start
  29.4 0.7 convert_element_type.31
  30.1 0.7 maximum_bitcast_fusion
  30.8 36.2 %all-gather = f32[512,128]{1,0:T(8,128)S(1)} all-gather(f32[16,128]{1,0:T(8,128)S(1)} %maximum_bitcast_fusion), channel_id=2, replica_groups=mesh['expert'=32,'tensor'=16] {'expert'}, dimensions={0}, use_global_device_ids=true | all-gather | bytes 270336 | tf_op jit(solution)/shard_map/all_gather | solution.py:24
  67.0 0.2 compare_reduce_fusion
  67.2 0.1 fusion.21
  67.4 37.3 %all-gather.9.cloned.1.call-done = bf16[4096,256]{1,0:T(8,128)(2,1)} async-done(((bf16[128,256]{1,0:T(8,128)(2,1)}), bf16[4096,256]{1,0:T(8,128)(2,1)}) %all-gather.9.cloned.1.call-update) | async-done | bytes 2097168 | tf_op jit(solution)/shard_map/all_gather | solution.py:25
  104.6 2.0 fusion
  106.7 1.0 copy.21
  107.6 0.0 all-gather.7.cloned.1.call-update
  107.7 0.0 reduce-scatter.3.cloned.1.call-start
  107.7 110.4 %all-gather.7.cloned.1.call-done = bf16[2,768,4096]{2,1,0:T(8,128)(2,1)} async-done(((bf16[2,768,256]{2,1,0:T(8,128)(2,1)}), bf16[2,768,4096]{2,1,0:T(8,128)(2,1)}) %all-gather.7.cloned.1.call-update) | async-done | bytes 12582928 | tf_op jit(solution)/shard_map/all_gather | solution.py:46
  218.2 9.0 %fusion.26 = f32[2,768,96]{1,2,0:T(8,128)S(1)} fusion(bf16[2,768,4096]{2,1,0:T(8,128)(2,1)} %all-gather.7.cloned.1.call-done, bf16[2,96,4096]{2,1,0:T(8,128)(2,1)} %param.11), kind=kOutput, calls=%fused_computation.36 | convolution fusion | flops 1207959552 | bytes 14745600 | tf_op jit(solution)/shard_map/erd,efd->erf/dot_general | solution.py:47
  227.1 0.0 copy-done
  227.1 15.3 %convolution_convert_fusion = bf16[2,768,4096]{2,1,0:T(8,128)(2,1)} fusion(bf16[2,96,4096]{2,1,0:T(8,128)(2,1)S(1)} %copy-done, bf16[2,768,4096]{2,1,0:T(8,128)(2,1)} %all-gather.7.cloned.1.call-done, bf16[2,96,4096]{2,1,0:T(8,128)(2,1)} %param.12, f32[2,768,96]{1,2,0:T(8,128)S(1)} %fusion.26), kind=kOutput, calls=%fused_computation | convolution fusion | flops 2423095296 | bytes 28901376 | tf_op jit(solution)/shard_map/erf,efd->erd/dot_general | solution.py:50
  242.4 0.0 reduce-scatter.3.cloned.1.call-update
  242.5 0.0 reduce-scatter.5.cloned.1.call-start
  242.5 0.2 fusion.16
  242.7 108.8 %reduce-scatter.3.cloned.1.call-done = bf16[2,768,256]{2,1,0:T(8,128)(2,1)} async-done(((bf16[2,768,4096]{2,1,0:T(8,128)(2,1)}), bf16[2,768,256]{2,1,0:T(8,128)(2,1)}) %reduce-scatter.3.cloned.1.call-update) | async-done | bytes 786448 | tf_op jit(solution)/shard_map/reduce_scatter | solution.py:53
  351.5 5.3 %multiply_reduce_fusion = bf16[32,128,256]{2,1,0:T(8,128)(2,1)} fusion(f32[32,2,128]{2,1,0:T(2,128)S(1)} %fusion.16, bf16[2,32,24,256]{3,2,1,0:T(8,128)(2,1)} %bitcast.27, f32[32,2,128]{2,1,0:T(2,128)S(1)} %copy.20, pred[32,2,128]{2,1,0:T(4,128)(4,1)S(1)} %compare_reduce_fusion), kind=kOutput, calls=%fused_computation.1 | convolution fusion | flops 104202240 | bytes 2957312 | tf_op jit(solution)/shard_map/bjst,jbsd->bjtd/dot_general | solution.py:55
  356.8 0.0 reduce-scatter.5.cloned.1.call-update
  356.9 111.2 %reduce-scatter.5.cloned.1.call-done = bf16[1,128,256]{2,1,0:T(8,128)(2,1)} async-done(((bf16[32,128,256]{2,1,0:T(8,128)(2,1)}), bf16[1,128,256]{2,1,0:T(8,128)(2,1)}) %reduce-scatter.5.cloned.1.call-update) | async-done | bytes 65552 | tf_op jit(solution)/shard_map/reduce_scatter | solution.py:57
  (5 shorter events, 0.1 us)
Async XLA Ops:
  6.5 220.6 %copy-start = (bf16[2,96,4096]{2,1,0:T(8,128)(2,1)S(1)}, bf16[2,96,4096]{2,1,0:T(8,128)(2,1)}, u32[]{:S(2)}) copy-start(bf16[2,96,4096]{2,1,0:T(8,128)(2,1)} %param.13) | copy-start | bytes 4718596
  6.5 98.1 %all-gather.9.cloned.1.call-start = ((), (), s32[]{:S(2)}) async-start(), calls=%async_computation.5 | async-start | bytes 2162688 | tf_op jit(solution)/shard_map/all_gather | solution.py:25
  29.3 188.8 %all-gather.7.cloned.1.call-start = ((), (), s32[]{:S(2)}) async-start(), calls=%async_computation.2 | async-start | bytes 13369344 | tf_op jit(solution)/shard_map/all_gather | solution.py:46
  107.7 243.9 %reduce-scatter.3.cloned.1.call-start = ((), (), s32[]{:S(2)}) async-start(), calls=%async_computation.3 | async-start | bytes 13369344 | tf_op jit(solution)/shard_map/reduce_scatter | solution.py:53
  242.5 225.6 %reduce-scatter.5.cloned.1.call-start = ((), (), s32[]{:S(2)}) async-start(), calls=%async_computation.4 | async-start | bytes 2162688 | tf_op jit(solution)/shard_map/reduce_scatter | solution.py:57
Sparse Core Ops, SparseCore 0:
  29.5 75.1 all-gather.8
  107.8 110.3 all-gather.6
  242.6 108.8 reduce-scatter.2
  357.0 111.0 reduce-scatter.4
